TPU v7x, 32 devices: a whole 2x2x4 slice. The times are simulated.
32 devices in a mesh: dp: 8 (over y, x, core), tensor: 4 (over z).
Axes of the slice: x: 2, y: 2, z: 4, core: 2. Of those that a mesh axis runs over, the one named last changes fastest.
Arguments:
- inputs: bfloat16 [16384, 768], P(('dp', 'tensor')), may hold values from -6 to 6
- out_grad: bfloat16 [16384, 768], P(('dp', 'tensor')), may hold values from -6 to 6
- seq_lengths: int32 [8, 3], P('dp'), may hold values from 1 to 1024, 2048 in all within a row
- balance: int32 [8, 2048], P('dp'), may hold values from 0 to 2047, each once within a row
- clusters: int32 [8, 12, 2048], P('dp', 'tensor'), may hold values from 0 to 2047, each once within a row
- query_weight: bfloat16 [768, 768], P('dp', 'tensor'), may hold values from -0.21875 to 0.21875
- query_bias: float32 [768], P('tensor'), may hold values from -3 to 3
- key_weight: bfloat16 [768, 768], P('dp', 'tensor'), may hold values from -0.21875 to 0.21875
- value_weight: bfloat16 [768, 768], P('dp', 'tensor'), may hold values from -0.21875 to 0.21875
- value_bias: float32 [768], P('tensor'), may hold values from -3 to 3
- out_weight: bfloat16 [768, 768], P('tensor', 'dp'), may hold values from -0.875 to 0.875
- out_bias: float32 [768], replicated, may hold values from -3 to 3
- norm1_gain: float32 [768], replicated, may hold values from 0.1 to 1.9
- norm1_bias: float32 [768], replicated, may hold values from -3 to 3
- up_weight: bfloat16 [768, 3072], P('dp', 'tensor'), may hold values from -0.21875 to 0.21875
- up_bias: float32 [3072], P('tensor'), may hold values from -3 to 3
- down_weight: bfloat16 [3072, 768], P('tensor', 'dp'), may hold values from -0.109375 to 0.109375
- down_bias: float32 [768], replicated, may hold values from -3 to 3
- norm2_gain: float32 [768], replicated, may hold values from 0.1 to 1.9
- norm2_bias: float32 [768], replicated, may hold values from -3 to 3
Outputs:
- layer_out: bfloat16 [16384, 768], P(('dp', 'tensor'))
- grad_inputs: float32 [16384, 768], P(('dp', 'tensor'))
- grad_query_weight: float32 [768, 768], P('dp', 'tensor')
- grad_query_bias: float32 [768], P('tensor')
- grad_key_weight: float32 [768, 768], P('dp', 'tensor')
- grad_value_weight: float32 [768, 768], P('dp', 'tensor')
- grad_value_bias: float32 [768], P('tensor')
- grad_out_weight: float32 [768, 768], P('tensor', 'dp')
- grad_out_bias: float32 [768], replicated
- grad_norm1_gain: float32 [768], replicated
- grad_norm1_bias: float32 [768], replicated
- grad_up_weight: float32 [768, 3072], P('dp', 'tensor')
- grad_up_bias: float32 [3072], P('tensor')
- grad_down_weight: float32 [3072, 768], P('tensor', 'dp')
- grad_down_bias: float32 [768], replicated
- grad_norm2_gain: float32 [768], replicated
- grad_norm2_bias: float32 [768], replicated
Inputs may be any that keep to these rules, and one draw needn't show every extreme that they name: `seq_lengths`: each group's lengths sum to 2048; the largest in each group is exactly 1024. `balance`: each group's row is a permutation of its 2048 token indices. `clusters`: each head's row of a group is a permutation of the 2048 balanced positions.
All inputs are finite; a program needn't handle non-finite values.
Results may differ from a plain program's by a relative error of at most 0.019.
Values may be sent and summed in bfloat16 or wider, within the bound.
No kernel may reach another device: no remote copies, remote signals or barrier semaphores. Data moves between devices by JAX's collectives and lax.ppermute only.
A program may use at most 128 MiB of HBM per device.

v0:
```python
import jax
import jax.numpy as jnp
from jax import lax
from jax.sharding import PartitionSpec as P

HD = 64
CL = 128


def layer_norm(values_in, gain, shift):
    center = values_in - jnp.mean(values_in, axis=-1, keepdims=True)
    variance = jnp.mean(center * center, axis=-1, keepdims=True)
    return center * lax.rsqrt(variance + 1e-06) * gain + shift


def gelu_tanh(values_in):
    return jax.nn.gelu(values_in, approximate=True)


def product(left, right):
    return jnp.dot(left, right, preferred_element_type=jnp.float32)


def product_nt(left, right):
    return lax.dot_general(
        left, right, (((1,), (1,)), ((), ())), preferred_element_type=jnp.float32
    )


def product_tn(left, right):
    return lax.dot_general(
        left, right, (((0,), (0,)), ((), ())), preferred_element_type=jnp.float32
    )


def to_slots(values_in, slot_order):
    token_count = values_in.shape[0]
    head_count = slot_order.shape[0]
    per_head = values_in.reshape(token_count, head_count, HD).transpose(1, 0, 2)
    picked = jnp.take_along_axis(per_head, slot_order[:, :, None], axis=1)
    return picked.reshape(head_count, token_count // CL, CL, HD)


def to_tokens(slots, token_place):
    head_count = slots.shape[0]
    flat_slots = slots.reshape(head_count, -1, HD)
    placed = jnp.take_along_axis(flat_slots, token_place[:, :, None], axis=1)
    return placed.transpose(1, 0, 2).reshape(flat_slots.shape[1], head_count * HD)


def masked_scores(query_slots, key_slots, segment_slots):
    raw_scores = jnp.einsum(
        "hcqd,hckd->hcqk", query_slots, key_slots, preferred_element_type=jnp.float32
    ) * HD ** (-0.5)
    same_doc = segment_slots[:, :, :, None] == segment_slots[:, :, None, :]
    return jnp.where(same_doc, raw_scores, -1e30)


def local(
    inputs,
    out_grad,
    seq_lengths,
    balance,
    clusters,
    query_weight,
    query_bias,
    key_weight,
    value_weight,
    value_bias,
    out_weight,
    out_bias,
    norm1_gain,
    norm1_bias,
    up_weight,
    up_bias,
    down_weight,
    down_bias,
    norm2_gain,
    norm2_bias,
):
    row_count = inputs.shape[0]
    tensor_size = lax.axis_size("tensor")
    tensor_rank = lax.axis_index("tensor")
    group_rows = row_count * tensor_size
    local_width = query_weight.shape[1]
    local_hidden = up_weight.shape[1]
    query_full, key_full, value_full, out_full, up_rows, down_cols = (
        lax.all_gather(query_weight, "dp", axis=0, tiled=True),
        lax.all_gather(key_weight, "dp", axis=0, tiled=True),
        lax.all_gather(value_weight, "dp", axis=0, tiled=True),
        lax.all_gather(out_weight, "dp", axis=1, tiled=True),
        lax.all_gather(up_weight, "dp", axis=0, tiled=True),
        lax.all_gather(down_weight, "dp", axis=1, tiled=True),
    )
    positions = jnp.arange(group_rows, dtype=jnp.int32)
    bounds = jnp.cumsum(seq_lengths[0])
    segment = jnp.sum((positions[:, None] >= bounds[None, :]).astype(jnp.int32), axis=1)
    slot_order = jnp.take(balance[0], clusters[0], axis=0)
    token_place = jax.vmap(
        lambda row_order: jnp.zeros((group_rows,), jnp.int32).at[row_order].set(positions)
    )(slot_order)
    segment_slots = jnp.take(segment, slot_order, axis=0).reshape(
        slot_order.shape[0], group_rows // CL, CL
    )
    inputs_all = lax.all_gather(inputs, "tensor", axis=0, tiled=True)
    query_rows = (product(inputs_all, query_full) + query_bias).astype(jnp.bfloat16)
    key_rows = product(inputs_all, key_full).astype(jnp.bfloat16)
    value_rows = (product(inputs_all, value_full) + value_bias).astype(jnp.bfloat16)
    query_slots = to_slots(query_rows, slot_order)
    key_slots = to_slots(key_rows, slot_order)
    value_slots = to_slots(value_rows, slot_order)
    scores = masked_scores(query_slots, key_slots, segment_slots)
    top_score = jnp.max(scores, axis=-1, keepdims=True)
    log_total = top_score + jnp.log(jnp.sum(jnp.exp(scores - top_score), axis=-1, keepdims=True))
    prob_low = jnp.exp(scores - log_total).astype(jnp.bfloat16)
    context_slots = jnp.einsum(
        "hcqk,hckd->hcqd", prob_low, value_slots, preferred_element_type=jnp.float32
    ).astype(jnp.bfloat16)
    context = to_tokens(context_slots, token_place)
    attention = lax.psum_scatter(
        product(context, out_full).astype(jnp.bfloat16), "tensor", scatter_dimension=0, tiled=True
    ).astype(jnp.float32)
    summed = inputs.astype(jnp.float32) + attention + out_bias
    normed = layer_norm(summed, norm1_gain, norm1_bias)
    normed_low = normed.astype(jnp.bfloat16)
    normed_all = lax.all_gather(normed_low, "tensor", axis=0, tiled=True)
    up_value = product(normed_all, up_rows) + up_bias
    active = gelu_tanh(up_value).astype(jnp.bfloat16)
    feed = lax.psum_scatter(
        product(active, down_cols).astype(jnp.bfloat16), "tensor", scatter_dimension=0, tiled=True
    ).astype(jnp.float32)
    pre_norm = normed + feed + down_bias
    layer_out = layer_norm(pre_norm, norm2_gain, norm2_bias).astype(jnp.bfloat16)
    _, norm2_pull = jax.vjp(layer_norm, pre_norm, norm2_gain, norm2_bias)
    grad_pre, grad_gain_two, grad_shift_two = norm2_pull(out_grad.astype(jnp.float32))
    grad_pre_low = grad_pre.astype(jnp.bfloat16)
    _, gelu_pull = jax.vjp(gelu_tanh, up_value)
    grad_pre_all = lax.all_gather(grad_pre_low, "tensor", axis=0, tiled=True)
    grad_up = gelu_pull(product_nt(grad_pre_all, down_cols))[0].astype(jnp.bfloat16)
    grad_down_local = product_tn(active, grad_pre_all)
    grad_up_local = product_tn(normed_all, grad_up)
    grad_normed_part = lax.psum_scatter(
        product_nt(grad_up, up_rows).astype(jnp.bfloat16), "tensor", scatter_dimension=0, tiled=True
    ).astype(jnp.float32)
    grad_up_bias_full = lax.dynamic_update_slice(
        jnp.zeros((local_hidden * tensor_size,), jnp.float32),
        jnp.sum(grad_up.astype(jnp.float32), axis=0),
        (tensor_rank * local_hidden,),
    )
    grad_normed = grad_pre + grad_normed_part
    _, norm1_pull = jax.vjp(layer_norm, summed, norm1_gain, norm1_bias)
    grad_summed, grad_gain_one, grad_shift_one = norm1_pull(grad_normed)
    grad_summed_low = grad_summed.astype(jnp.bfloat16)
    grad_summed_all = lax.all_gather(grad_summed_low, "tensor", axis=0, tiled=True)
    grad_out_local = product_tn(context, grad_summed_all)
    grad_context = product_nt(grad_summed_all, out_full).astype(jnp.bfloat16)
    grad_context_slots = to_slots(grad_context, slot_order)
    again_scores = masked_scores(query_slots, key_slots, segment_slots)
    prob_values = jnp.exp(again_scores - log_total)
    again_low = prob_values.astype(jnp.bfloat16)
    grad_prob = jnp.einsum(
        "hcqd,hckd->hcqk", grad_context_slots, value_slots, preferred_element_type=jnp.float32
    )
    grad_scores = (
        prob_values * (grad_prob - jnp.sum(prob_values * grad_prob, axis=-1, keepdims=True))
    ).astype(jnp.bfloat16)
    grad_query_slots = (
        jnp.einsum("hcqk,hckd->hcqd", grad_scores, key_slots, preferred_element_type=jnp.float32)
        * HD ** (-0.5)
    ).astype(jnp.bfloat16)
    grad_key_slots = (
        jnp.einsum("hcqk,hcqd->hckd", grad_scores, query_slots, preferred_element_type=jnp.float32)
        * HD ** (-0.5)
    ).astype(jnp.bfloat16)
    grad_value_slots = jnp.einsum(
        "hcqk,hcqd->hckd", again_low, grad_context_slots, preferred_element_type=jnp.float32
    ).astype(jnp.bfloat16)
    grad_query = to_tokens(grad_query_slots, token_place)
    grad_key = to_tokens(grad_key_slots, token_place)
    grad_value = to_tokens(grad_value_slots, token_place)
    grad_query_local = product_tn(inputs_all, grad_query)
    grad_key_local = product_tn(inputs_all, grad_key)
    grad_value_local = product_tn(inputs_all, grad_value)
    grad_inputs = grad_summed + lax.psum_scatter(
        (
            product_nt(grad_query, query_full)
            + product_nt(grad_key, key_full)
            + product_nt(grad_value, value_full)
        ).astype(jnp.bfloat16),
        "tensor",
        scatter_dimension=0,
        tiled=True,
    ).astype(jnp.float32)
    width_full = local_width * tensor_size

    def spread_width(part_sum):
        return lax.dynamic_update_slice(
            jnp.zeros((width_full,), jnp.float32), part_sum, (tensor_rank * local_width,)
        )

    (
        query_bias_sum,
        value_bias_sum,
        up_bias_sum,
        grad_out_bias,
        grad_norm1_gain,
        grad_norm1_bias,
        grad_down_bias,
        grad_norm2_gain,
        grad_norm2_bias,
    ) = lax.psum(
        (
            spread_width(jnp.sum(grad_query.astype(jnp.float32), axis=0)),
            spread_width(jnp.sum(grad_value.astype(jnp.float32), axis=0)),
            grad_up_bias_full,
            jnp.sum(grad_summed, axis=0),
            grad_gain_one,
            grad_shift_one,
            jnp.sum(grad_pre, axis=0),
            grad_gain_two,
            grad_shift_two,
        ),
        ("dp", "tensor"),
    )
    grad_query_bias = lax.dynamic_slice_in_dim(
        query_bias_sum, tensor_rank * local_width, local_width, 0
    )
    grad_value_bias = lax.dynamic_slice_in_dim(
        value_bias_sum, tensor_rank * local_width, local_width, 0
    )
    grad_up_bias = lax.dynamic_slice_in_dim(
        up_bias_sum, tensor_rank * local_hidden, local_hidden, 0
    )
    (
        grad_query_weight,
        grad_key_weight,
        grad_value_weight,
        grad_out_weight,
        grad_up_weight,
        grad_down_weight,
    ) = (
        lax.psum_scatter(grad_query_local, "dp", scatter_dimension=0, tiled=True),
        lax.psum_scatter(grad_key_local, "dp", scatter_dimension=0, tiled=True),
        lax.psum_scatter(grad_value_local, "dp", scatter_dimension=0, tiled=True),
        lax.psum_scatter(grad_out_local, "dp", scatter_dimension=1, tiled=True),
        lax.psum_scatter(grad_up_local, "dp", scatter_dimension=0, tiled=True),
        lax.psum_scatter(grad_down_local, "dp", scatter_dimension=1, tiled=True),
    )
    return (
        layer_out,
        grad_inputs,
        grad_query_weight,
        grad_query_bias,
        grad_key_weight,
        grad_value_weight,
        grad_value_bias,
        grad_out_weight,
        grad_out_bias,
        grad_norm1_gain,
        grad_norm1_bias,
        grad_up_weight,
        grad_up_bias,
        grad_down_weight,
        grad_down_bias,
        grad_norm2_gain,
        grad_norm2_bias,
    )


def solution(mesh):
    in_specs = (
        P(("dp", "tensor"), None),
        P(("dp", "tensor"), None),
        P("dp", None),
        P("dp", None),
        P("dp", "tensor", None),
        P("dp", "tensor"),
        P("tensor"),
        P("dp", "tensor"),
        P("dp", "tensor"),
        P("tensor"),
        P("tensor", "dp"),
        P(),
        P(),
        P(),
        P("dp", "tensor"),
        P("tensor"),
        P("tensor", "dp"),
        P(),
        P(),
        P(),
    )
    out_specs = (
        P(("dp", "tensor"), None),
        P(("dp", "tensor"), None),
        P("dp", "tensor"),
        P("tensor"),
        P("dp", "tensor"),
        P("dp", "tensor"),
        P("tensor"),
        P("tensor", "dp"),
        P(),
        P(),
        P(),
        P("dp", "tensor"),
        P("tensor"),
        P("tensor", "dp"),
        P(),
        P(),
        P(),
    )
    return jax.shard_map(local, mesh=mesh, in_specs=in_specs, out_specs=out_specs, check_vma=False)
```

profile of v0, /device:TPU:0, one launch (start us, length us, event | category | flops | bytes accessed | tf_op | source)
XLA Modules:
  0.0 1201.1 jit_solution(17774574574458499164)
XLA Ops:
  9.7 34.3 %gather_fusion = s32[6144]{0:T(1024)S(1)} fusion(s32[2048]{0:T(1024)S(1)} %bitcast.160, s32[6144]{0:T(1024)S(1)} %broadcast_clamp_fusion.1), kind=kCustom, calls=%fused_computation.clone | custom fusion | bytes 73728 | tf_op jit(solution)/shard_map/jit(_take)/gather | solution.py:98
  44.6 23.0 %scatter_custom_fusion = s32[6144]{0:T(1024)S(1)} fusion(s32[6144]{0:T(1024)S(1)} %reshape.282, s32[6144]{0:T(1024)S(1)} %reshape.284, s32[]{:T(128)} %constant.20.clone.1), kind=kCustom, calls=%fused_computation.120 | custom fusion | bytes 24580
  67.9 34.3 %gather_fusion.1 = s32[6144]{0:T(1024)S(1)} fusion(s32[2048]{0:T(1024)S(1)} %convert_reduce_fusion.4, s32[6144]{0:T(1024)S(1)} %broadcast_clamp_fusion), kind=kCustom, calls=%fused_computation.2.clone | custom fusion | bytes 73728 | tf_op jit(solution)/shard_map/jit(_take)/gather | solution.py:102
  102.4 12.1 %all_gather.34 = bf16[192,768]{0,1:T(8,128)(2,1)} all-gather(bf16[192,96]{0,1:T(8,128)(2,1)S(1)} %copy.132), channel_id=1, replica_groups=mesh['dp'=8,'tensor'=4] {'dp'}, dimensions={1}, use_global_device_ids=true | all-gather | bytes 331776 | tf_op jit(solution)/shard_map/all_gather | solution.py:91
  114.5 10.5 all_gather.31
  124.9 9.6 all_gather.32
  134.6 9.7 all_gather.33
  144.3 3.1 fusion.8
  148.3 32.3 %gather_fusion.4 = bf16[6144,64]{1,0:T(8,128)(2,1)S(1)} fusion(bf16[3,2048,64]{2,1,0:T(8,128)(2,1)S(1)} %bitcast.163, s32[6144]{0:T(1024)S(1)} %reshape.300), kind=kCustom, calls=%fused_computation.4.clone | custom fusion | bytes 1622016 | tf_op jit(solution)/shard_map/jit(take_along_axis)/gather | solution.py:40
  182.0 3.1 convolution_convert_fusion.4
  186.0 32.3 %gather_fusion.3 = bf16[6144,64]{1,0:T(8,128)(2,1)S(1)} fusion(bf16[3,2048,64]{2,1,0:T(8,128)(2,1)S(1)} %bitcast.164, s32[6144]{0:T(1024)S(1)} %reshape.300), kind=kCustom, calls=%fused_computation.3.clone | custom fusion | bytes 1622016 | tf_op jit(solution)/shard_map/jit(take_along_axis)/gather | solution.py:40
  219.7 3.1 fusion.7
  223.7 32.3 %gather_fusion.2 = bf16[6144,64]{1,0:T(8,128)(2,1)S(1)} fusion(bf16[3,2048,64]{2,1,0:T(8,128)(2,1)S(1)} %bitcast.165, s32[6144]{0:T(1024)S(1)} %reshape.300), kind=kCustom, calls=%fused_computation.1.clone | custom fusion | bytes 1622016 | tf_op jit(solution)/shard_map/jit(take_along_axis)/gather | solution.py:40
  256.7 1.6 select_bitcast_fusion.3
  258.3 3.2 fusion.46
  264.6 32.3 %gather_fusion.5 = bf16[6144,64]{1,0:T(8,128)(2,1)S(1)} fusion(bf16[3,2048,64]{2,1,0:T(8,128)(2,1)S(1)} %bitcast.166, s32[6144]{0:T(1024)S(1)} %reshape.312), kind=kCustom, calls=%fused_computation.5.clone | custom fusion | bytes 1622016 | tf_op jit(solution)/shard_map/jit(take_along_axis)/gather | solution.py:47
  298.6 2.7 convolution_convert_fusion.2
  302.2 59.9 %reduce-scatter.19.cloned.1.call-done = bf16[512,768]{1,0:T(8,128)(2,1)} async-done(((bf16[2048,768]{1,0:T(8,128)(2,1)}), bf16[512,768]{1,0:T(8,128)(2,1)}) %reduce-scatter.19.cloned.1.call-update) | async-done | bytes 786448 | tf_op jit(solution)/shard_map/reduce_scatter | solution.py:120
  362.1 1.5 fusion.15
  363.6 1.6 multiply_reduce_fusion.4
  367.3 62.8 %all-gather.9.cloned.1.call-done = bf16[2048,768]{1,0:T(8,128)(2,1)} async-done(((bf16[512,768]{1,0:T(8,128)(2,1)}), bf16[2048,768]{1,0:T(8,128)(2,1)}) %all-gather.9.cloned.1.call-update) | async-done | bytes 3145744 | tf_op jit(solution)/shard_map/all_gather | solution.py:126
  430.1 9.7 multiply_convert_fusion
  439.8 14.6 %all-gather.13.cloned.1.call-done = bf16[768,768]{0,1:T(8,128)(2,1)} async-done(((bf16[768,96]{0,1:T(8,128)(2,1)}), bf16[768,768]{0,1:T(8,128)(2,1)}) %all-gather.13.cloned.1.call-update) | async-done | bytes 1179664 | tf_op jit(solution)/shard_map/all_gather | solution.py:93
  454.4 6.5 convolution_convert_fusion.1
  461.0 60.3 %reduce-scatter.21.cloned.1.call-done = bf16[512,768]{1,0:T(8,128)(2,1)} async-done(((bf16[2048,768]{1,0:T(8,128)(2,1)}), bf16[512,768]{1,0:T(8,128)(2,1)}) %reduce-scatter.21.cloned.1.call-update) | async-done | bytes 786448 | tf_op jit(solution)/shard_map/reduce_scatter | solution.py:129
  521.3 1.9 fusion.45
  524.3 2.7 fusion.44
  528.3 63.3 %all-gather.15.cloned.1.call-done = bf16[2048,768]{1,0:T(8,128)(2,1)} async-done(((bf16[512,768]{1,0:T(8,128)(2,1)}), bf16[2048,768]{1,0:T(8,128)(2,1)}) %all-gather.15.cloned.1.call-update) | async-done | bytes 3145744 | tf_op jit(solution)/shard_map/all_gather | solution.py:138
  591.6 8.8 convert_reduce_fusion
  600.4 1.6 copy-done.52
  602.1 4.0 convolution_convert_fusion
  606.2 59.0 %reduce-scatter.23.cloned.1.call-done = bf16[512,768]{1,0:T(8,128)(2,1)} async-done(((bf16[2048,768]{1,0:T(8,128)(2,1)}), bf16[512,768]{1,0:T(8,128)(2,1)}) %reduce-scatter.23.cloned.1.call-update) | async-done | bytes 786448 | tf_op jit(solution)/shard_map/reduce_scatter | solution.py:142
  665.2 2.2 multiply_reduce_fusion.1
  671.2 63.1 %all-gather.17.cloned.1.call-done = bf16[2048,768]{1,0:T(8,128)(2,1)} async-done(((bf16[512,768]{1,0:T(8,128)(2,1)}), bf16[2048,768]{1,0:T(8,128)(2,1)}) %all-gather.17.cloned.1.call-update) | async-done | bytes 3145744 | tf_op jit(solution)/shard_map/all_gather | solution.py:154
  734.3 3.1 convolution_convert_fusion.3
  738.2 60.6 %gather_fusion.6 = bf16[6144,64]{1,0:T(8,128)(2,1)} fusion(bf16[3,2048,64]{2,1,0:T(8,128)(2,1)S(1)} %bitcast.161, s32[6144]{0:T(1024)S(1)} %reshape.300), kind=kCustom, calls=%fused_computation.6.clone | custom fusion | bytes 1622016 | tf_op jit(solution)/shard_map/jit(take_along_axis)/gather | solution.py:40
  798.8 2.6 copy.134
  801.4 4.3 convolution_convert_fusion.6
  807.9 2.1 multiply_convert_fusion.2
  809.9 1.5 multiply_convert_fusion.3
  811.4 2.2 convolution_bitcast_fusion
  814.8 32.3 %gather_fusion.9 = bf16[6144,64]{1,0:T(8,128)(2,1)S(1)} fusion(bf16[3,2048,64]{2,1,0:T(8,128)(2,1)S(1)} %bitcast.167, s32[6144]{0:T(1024)S(1)} %reshape.312), kind=kCustom, calls=%fused_computation.9.clone | custom fusion | bytes 1622016 | tf_op jit(solution)/shard_map/jit(take_along_axis)/gather | solution.py:47
  848.5 1.8 copy.160
  850.3 32.3 %gather_fusion.7 = bf16[6144,64]{1,0:T(8,128)(2,1)S(1)} fusion(bf16[3,2048,64]{2,1,0:T(8,128)(2,1)S(1)} %bitcast.168, s32[6144]{0:T(1024)S(1)} %reshape.312), kind=kCustom, calls=%fused_computation.7.clone | custom fusion | bytes 1622016 | tf_op jit(solution)/shard_map/jit(take_along_axis)/gather | solution.py:47
  884.0 1.8 copy.161
  885.8 32.3 %gather_fusion.8 = bf16[6144,64]{1,0:T(8,128)(2,1)S(1)} fusion(bf16[3,2048,64]{2,1,0:T(8,128)(2,1)S(1)} %bitcast.162, s32[6144]{0:T(1024)S(1)} %reshape.312), kind=kCustom, calls=%fused_computation.8.clone | custom fusion | bytes 1622016 | tf_op jit(solution)/shard_map/jit(take_along_axis)/gather | solution.py:47
  922.7 2.8 add_convert_fusion
  925.5 1.8 copy-done.46
  927.3 6.0 fusion.49
  933.6 7.1 fusion.50
  940.8 2.8 convolution_bitcast_fusion.1
  943.6 2.2 copy.167
  945.9 2.8 convolution_bitcast_fusion.3
  948.7 2.2 copy.163
  951.0 2.8 convolution_bitcast_fusion.2
  953.7 2.3 copy.165
  957.0 43.1 %all-reduce = (f32[768]{0:T(1024)S(1)}, f32[768]{0:T(1024)S(1)}, f32[768]{0:T(1024)}, f32[768]{0:T(1024)}, f32[768]{0:T(1024)}, /*index=5*/f32[3072]{0:T(1024)S(1)}, f32[768]{0:T(1024)}, f32[768]{0:T(1024)}, f32[768]{0:T(1024)}) all-reduce(f32[768]{0:T(1024)S(1)} %dynamic_update_slice.9, ...), channel_id=1, replica_groups=mesh['dp'=8,'tensor'=4] {'dp','tensor'}, use_global_device_ids=true, to_apply=%region_20.23 | all-reduce | flops 9216 | bytes 73728 | tf_op jit(solution)/shard_map/psum | solution.py:211
  1002.0 1.6 copy.170
  1003.6 2.5 convert_add_fusion
  1006.2 25.1 %reduce-scatter.27.cloned.1.call-done = f32[96,768]{1,0:T(8,128)} async-done(((f32[768,768]{1,0:T(8,128)}), f32[96,768]{1,0:T(8,128)}) %reduce-scatter.27.cloned.1.call-update) | async-done | bytes 294928 | tf_op jit(solution)/shard_map/reduce_scatter | solution.py:246
  1031.3 46.5 %reduce-scatter.29.cloned.1.call-done = f32[768,96]{0,1:T(8,128)} async-done(((f32[768,768]{0,1:T(8,128)}), f32[768,96]{0,1:T(8,128)}) %reduce-scatter.29.cloned.1.call-update) | async-done | bytes 294928 | tf_op jit(solution)/shard_map/reduce_scatter | solution.py:247
  1077.8 38.7 %reduce-scatter.35.cloned.1.call-done = f32[96,192]{1,0:T(8,128)} async-done(((f32[768,192]{1,0:T(8,128)}), f32[96,192]{1,0:T(8,128)}) %reduce-scatter.35.cloned.1.call-update) | async-done | bytes 73744
  1116.5 38.5 %reduce-scatter.31.cloned.1.call-done = f32[96,192]{1,0:T(8,128)} async-done(((f32[768,192]{1,0:T(8,128)}), f32[96,192]{1,0:T(8,128)}) %reduce-scatter.31.cloned.1.call-update) | async-done | bytes 73744
  1155.0 38.7 %reduce-scatter.33.cloned.1.call-done = f32[96,192]{1,0:T(8,128)} async-done(((f32[768,192]{1,0:T(8,128)}), f32[96,192]{1,0:T(8,128)}) %reduce-scatter.33.cloned.1.call-update) | async-done | bytes 73744
  (216 shorter events, 37.3 us)
Async XLA Ops:
  8.0 1.6 copy-start
  8.0 136.3 %all-gather.7.cloned.1.call-start = ((), (), s32[]{:S(2)}) async-start(), calls=%async_computation.10 | async-start | bytes 3932160 | tf_op jit(solution)/shard_map/all_gather | solution.py:105
  8.8 353.3 %reduce-scatter.19.cloned.1.call-start = ((), (), s32[]{:S(2)}) async-start(), calls=%async_computation.11 | async-start | bytes 3932160 | tf_op jit(solution)/shard_map/reduce_scatter | solution.py:120
  9.6 34.4 %copy-start.34 = (s32[1,3,2048]{2,0,1:T(1,128)S(1)}, s32[1,3,2048]{2,0,1:T(1,128)}, u32[]{:S(2)}) copy-start(s32[1,3,2048]{2,0,1:T(1,128)} %param.28) | copy-start | bytes 73732
  9.6 34.5 %copy-start.44 = (s32[2]{0:T(128)S(1)}, s32[2]{0:T(128)}, u32[]{:S(2)}) copy-start(s32[2]{0:T(128)} %constant.77) | copy-start | bytes 28
  9.7 34.5 %copy-start.45 = (s32[2]{0:T(128)S(1)}, s32[2]{0:T(128)}, u32[]{:S(2)}) copy-start(s32[2]{0:T(128)} %constant.80) | copy-start | bytes 28
  9.7 34.7 %copy-start.51 = (s32[1,3]{1,0:T(1,128)S(1)}, s32[1,3]{1,0:T(1,128)}, u32[]{:S(2)}) copy-start(s32[1,3]{1,0:T(1,128)} %param.26) | copy-start | bytes 40
  67.9 34.4 %copy-start.39 = (bf16[192,96]{1,0:T(8,128)(2,1)S(1)}, bf16[192,96]{1,0:T(8,128)(2,1)}, u32[]{:S(2)}) copy-start(bf16[192,96]{1,0:T(8,128)(2,1)} %param.34) | copy-start | bytes 110596
  67.9 46.6 %copy-start.36 = (bf16[96,192]{1,0:T(8,128)(2,1)S(1)}, bf16[96,192]{1,0:T(8,128)(2,1)}, u32[]{:S(2)}) copy-start(bf16[96,192]{1,0:T(8,128)(2,1)} %param.29) | copy-start | bytes 110596
  67.9 57.0 %copy-start.37 = (bf16[96,192]{1,0:T(8,128)(2,1)S(1)}, bf16[96,192]{1,0:T(8,128)(2,1)}, u32[]{:S(2)}) copy-start(bf16[96,192]{1,0:T(8,128)(2,1)} %param.31) | copy-start | bytes 110596
  67.9 66.7 %copy-start.38 = (bf16[96,192]{1,0:T(8,128)(2,1)S(1)}, bf16[96,192]{1,0:T(8,128)(2,1)}, u32[]{:S(2)}) copy-start(bf16[96,192]{1,0:T(8,128)(2,1)} %param.32) | copy-start | bytes 110596
  67.9 76.4 %copy-start.49 = (f32[192]{0:T(256)S(1)}, f32[192]{0:T(256)}, u32[]{:S(2)}) copy-start(f32[192]{0:T(256)} %param.33) | copy-start | bytes 2308
  144.2 3.2 copy-start.31
  186.0 33.7 %copy-start.50 = (f32[192]{0:T(256)S(1)}, f32[192]{0:T(256)}, u32[]{:S(2)}) copy-start(f32[192]{0:T(256)} %param.30) | copy-start | bytes 2308
  258.3 3.9 copy-start.19
  258.3 3.9 copy-start.21
  258.3 3.9 copy-start.12
  261.5 1.7 copy-start.2
  296.9 1.7 copy-start.16
  298.6 63.5 %copy-start.5 = (bf16[512,768]{1,0:T(8,128)(2,1)S(1)}, bf16[512,768]{1,0:T(8,128)(2,1)}, u32[]{:S(2)}) copy-start(bf16[512,768]{1,0:T(8,128)(2,1)} %param.24) | copy-start | bytes 2359300
  298.6 63.5 %copy-start.33 = (f32[768]{0:T(1024)S(1)}, f32[768]{0:T(1024)}, u32[]{:S(2)}) copy-start(f32[768]{0:T(1024)} %param.35) | copy-start | bytes 9220
  301.3 63.9 %copy-start.35 = (f32[768]{0:T(1024)S(1)}, f32[768]{0:T(1024)}, u32[]{:S(2)}) copy-start(f32[768]{0:T(1024)} %param.36) | copy-start | bytes 9220
  301.3 63.9 %copy-start.41 = (f32[768]{0:T(1024)S(1)}, f32[768]{0:T(1024)}, u32[]{:S(2)}) copy-start(f32[768]{0:T(1024)} %param.37) | copy-start | bytes 9220
  301.3 65.9 %all-gather.11.cloned.1.call-start = ((), (), s32[]{:S(2)}) async-start(), calls=%async_computation.13 | async-start | bytes 1327104 | tf_op jit(solution)/shard_map/all_gather | solution.py:92
  301.9 128.1 %copy-start.48 = (f32[768]{0:T(1024)S(1)}, f32[768]{0:T(1024)}, u32[]{:S(2)}) copy-start(f32[768]{0:T(1024)} %param.39) | copy-start | bytes 9220
  301.9 128.1 %all-gather.9.cloned.1.call-start = ((), (), s32[]{:S(2)}) async-start(), calls=%async_computation.12 | async-start | bytes 3932160 | tf_op jit(solution)/shard_map/all_gather | solution.py:126
  362.1 3.2 copy-start.6
  366.6 87.8 %all-gather.13.cloned.1.call-start = ((), (), s32[]{:S(2)}) async-start(), calls=%async_computation.14 | async-start | bytes 1327104 | tf_op jit(solution)/shard_map/all_gather | solution.py:93
  367.2 154.1 %reduce-scatter.21.cloned.1.call-start = ((), (), s32[]{:S(2)}) async-start(), calls=%async_computation.15 | async-start | bytes 3932160 | tf_op jit(solution)/shard_map/reduce_scatter | solution.py:129
  460.9 60.4 %copy-start.43 = (f32[768]{0:T(1024)S(1)}, f32[768]{0:T(1024)}, u32[]{:S(2)}) copy-start(f32[768]{0:T(1024)} %param.41) | copy-start | bytes 9220
  460.9 62.6 %copy-start.18 = (bf16[512,768]{1,0:T(8,128)(2,1)S(1)}, bf16[512,768]{1,0:T(8,128)(2,1)}, u32[]{:S(2)}) copy-start(bf16[512,768]{1,0:T(8,128)(2,1)} %param.25) | copy-start | bytes 2359300
  461.0 62.6 %copy-start.40 = (f32[768]{0:T(1024)S(1)}, f32[768]{0:T(1024)}, u32[]{:S(2)}) copy-start(f32[768]{0:T(1024)} %param.42) | copy-start | bytes 9220
  461.0 63.3 %copy-start.42 = (f32[768]{0:T(1024)S(1)}, f32[768]{0:T(1024)}, u32[]{:S(2)}) copy-start(f32[768]{0:T(1024)} %param.43) | copy-start | bytes 9220
  461.0 130.6 %all-gather.15.cloned.1.call-start = ((), (), s32[]{:S(2)}) async-start(), calls=%async_computation.16 | async-start | bytes 3932160 | tf_op jit(solution)/shard_map/all_gather | solution.py:138
  528.0 137.1 %reduce-scatter.23.cloned.1.call-start = ((), (), s32[]{:S(2)}) async-start(), calls=%async_computation.17 | async-start | bytes 3932160 | tf_op jit(solution)/shard_map/reduce_scatter | solution.py:142
  591.6 10.4 copy-start.47
  600.4 1.6 copy-start.52
  606.1 128.2 %all-gather.17.cloned.1.call-start = ((), (), s32[]{:S(2)}) async-start(), calls=%async_computation.18 | async-start | bytes 3932160 | tf_op jit(solution)/shard_map/all_gather | solution.py:154
  665.2 2.3 copy-start.24
  668.4 1.2 copy-start.7
  668.4 65.9 %copy-start.17 = (bf16[192,768]{0,1:T(8,128)(2,1)S(1)}, bf16[192,768]{0,1:T(8,128)(2,1)}, u32[]{:S(2)}) copy-start(bf16[192,768]{0,1:T(8,128)(2,1)} %all_gather.34) | copy-start | bytes 884740
  670.7 331.3 %reduce-scatter.37.cloned.1.call-start = ((), (), s32[]{:S(2)}) async-start(), calls=%async_computation.25 | async-start | bytes 884736
  798.8 6.9 copy-start.3
  801.4 4.3 copy-start.13
  801.4 4.3 copy-start.14
  807.9 2.1 copy-start.20
  807.9 3.6 copy-start.25
  807.9 3.6 copy-start.29
  811.4 2.5 copy-start.23
  813.7 189.9 %reduce-scatter.25.cloned.1.call-start = ((), (), s32[]{:S(2)}) async-start(), calls=%async_computation.19 | async-start | bytes 3932160 | tf_op jit(solution)/shard_map/reduce_scatter | solution.py:184
  918.9 1.3 copy-start.9
  919.1 1.2 copy-start.26
  919.1 1.4 copy-start.27
  921.1 1.5 copy-start.10
  921.1 1.5 copy-start.11
  925.4 1.9 copy-start.46
  925.5 105.8 %reduce-scatter.27.cloned.1.call-start = ((), (), s32[]{:S(2)}) async-start(), calls=%async_computation.20 | async-start | bytes 2654208 | tf_op jit(solution)/shard_map/reduce_scatter | solution.py:246
  933.4 7.4 copy-start.4
  933.4 144.4 %reduce-scatter.29.cloned.1.call-start = ((), (), s32[]{:S(2)}) async-start(), calls=%async_computation.21 | async-start | bytes 2654208 | tf_op jit(solution)/shard_map/reduce_scatter | solution.py:247
  940.7 175.7 %reduce-scatter.35.cloned.1.call-start = ((), (), s32[]{:S(2)}) async-start(), calls=%async_computation.24 | async-start | bytes 884736
  945.8 209.2 %reduce-scatter.31.cloned.1.call-start = ((), (), s32[]{:S(2)}) async-start(), calls=%async_computation.22 | async-start | bytes 884736
  950.9 242.8 %reduce-scatter.33.cloned.1.call-start = ((), (), s32[]{:S(2)}) async-start(), calls=%async_computation.23 | async-start | bytes 884736
  951.0 242.8 %copy-start.1 = (s32[1,2048]{1,0:T(1,128)S(1)}, s32[1,2048]{1,0:T(1,128)}, u32[]{:S(2)}) copy-start(s32[1,2048]{1,0:T(1,128)} %param.27) | copy-start | bytes 24580
  953.7 49.9 %copy-start.8 = (f32[512,768]{1,0:T(8,128)S(1)}, f32[512,768]{1,0:T(8,128)}, u32[]{:S(2)}) copy-start(f32[512,768]{1,0:T(8,128)} %copy-done.7) | copy-start | bytes 4718596
  (5 other events, 5.2 us)
Sparse Core Ops, SparseCore 0:
  10.4 66.1 all-gather.6
  301.5 60.5 reduce-scatter.18
  528.2 63.4 all-gather.14
  670.9 63.4 all-gather.16
Sparse Core Ops, SparseCore 1:
  303.7 24.1 all-gather.10
  366.7 63.3 all-gather.8
  431.8 22.5 all-gather.12
  461.0 60.2 reduce-scatter.20
  606.2 58.9 reduce-scatter.22
  813.8 33.5 reduce-scatter.36
  925.5 59.6 reduce-scatter.24
  988.9 42.3 reduce-scatter.26
  1035.4 42.3 reduce-scatter.28
  1081.5 34.9 reduce-scatter.34
  1120.1 34.9 reduce-scatter.30
  1158.8 34.9 reduce-scatter.32
where the time goes:
time: 1210 us; the launch traced here: 1200 us
  waiting for transfers between devices  572 us (47%)
  local copies, waits for them, and re-layouts  417 us (34%)
  matrix products  85.4 us (7%)
  blocking collectives  84.9 us (7%)
  other arithmetic  23.4 us (2%)
  between operations  16.6 us (1%)
    gather x9, local copies, waits for them, and re-layouts, to_slots(): picked = jnp.take_along_axis(per_head, slot_order[:, :, None], axis=1)  164 us
    gather x9, local copies, waits for them, and re-layouts, to_tokens(): placed = jnp.take_along_axis(flat_slots, token_place[:, :, None], axis=1)  133 us
    unnamed x20, waiting for transfers between devices  118 us
    all_gather x1, waiting for transfers between devices, local(): grad_pre_all = lax.all_gather(grad_pre_low, 'tensor', axis=0, tiled=True)  63.3 us
    all_gather x1, waiting for transfers between devices, local(): lax.all_gather(grad_summed_low, 'tensor', axis=0, tiled=True)  63.1 us
    all_gather x1, waiting for transfers between devices, local(): normed_all = lax.all_gather(normed_low, 'tensor', axis=0, tiled=True)  62.8 us
    reduce_scatter x1, waiting for transfers between devices, local(): lax.psum_scatter(product(active, down_cols).astype(jnp.bfloat16), 'tensor...  60.3 us
    reduce_scatter x1, waiting for transfers between devices, local(): lax.psum_scatter(product(context, out_full).astype(jnp.bfloat16), 'tensor...  59.9 us
  transfers between devices with their start and end apart: 16, of which 12 were waited for; matrix products, arithmetic and copies ran while one was open for 21% of the time, Pallas kernels for 0%

commit v1 on v0

--- a/solution.py
+++ b/solution.py
@@ -1,3 +1,4 @@
+import functools
 import jax
 import jax.numpy as jnp
 from jax import lax
@@ -5,6 +6,15 @@
 
 HD = 64
 CL = 128
+
+
+def regions_tell(a0, axis_key, net_axis):
+    for nth in (axis_key, net_axis):
+        a0 = jax.lax.psum(a0, nth)
+    return a0
+
+
+_load_routes_all = functools.partial(regions_tell, axis_key="tensor", net_axis="dp")
 
 
 def layer_norm(values_in, gain, shift):
@@ -208,7 +218,7 @@
         grad_down_bias,
         grad_norm2_gain,
         grad_norm2_bias,
-    ) = lax.psum(
+    ) = _load_routes_all(
         (
             spread_width(jnp.sum(grad_query.astype(jnp.float32), axis=0)),
             spread_width(jnp.sum(grad_value.astype(jnp.float32), axis=0)),
@@ -219,8 +229,7 @@
             jnp.sum(grad_pre, axis=0),
             grad_gain_two,
             grad_shift_two,
-        ),
-        ("dp", "tensor"),
+        )
     )
     grad_query_bias = lax.dynamic_slice_in_dim(
         query_bias_sum, tensor_rank * local_width, local_width, 0

time: 1210 us -> 1210 us (level)
    psum x1 -> x2, blocking collectives: 43.1 us -> 42.9 us  [regions_tell(): a0 = jax.lax.psum(a0, nth)]
where the time goes in v1:
time: 1210 us; the launch traced here: 1200 us
  waiting for transfers between devices  573 us (47%)
  local copies, waits for them, and re-layouts  417 us (34%)
  matrix products  85.3 us (7%)
  blocking collectives  84.7 us (7%)
  other arithmetic  23.4 us (2%)
  between operations  16.6 us (1%)
    gather x9, local copies, waits for them, and re-layouts, to_slots(): picked = jnp.take_along_axis(per_head, slot_order[:, :, None], axis=1)  164 us
    gather x9, local copies, waits for them, and re-layouts, to_tokens(): placed = jnp.take_along_axis(flat_slots, token_place[:, :, None], axis=1)  133 us
    unnamed x20, waiting for transfers between devices  118 us
    all_gather x1, waiting for transfers between devices, local(): grad_pre_all = lax.all_gather(grad_pre_low, 'tensor', axis=0, tiled=True)  63.3 us
    all_gather x1, waiting for transfers between devices, local(): lax.all_gather(grad_summed_low, 'tensor', axis=0, tiled=True)  63.1 us
    all_gather x1, waiting for transfers between devices, local(): normed_all = lax.all_gather(normed_low, 'tensor', axis=0, tiled=True)  62.8 us
    reduce_scatter x1, waiting for transfers between devices, local(): lax.psum_scatter(product(active, down_cols).astype(jnp.bfloat16), 'tensor...  60.3 us
    reduce_scatter x1, waiting for transfers between devices, local(): lax.psum_scatter(product(context, out_full).astype(jnp.bfloat16), 'tensor...  59.9 us
  transfers between devices with their start and end apart: 16, of which 12 were waited for; matrix products, arithmetic and copies ran while one was open for 21% of the time, Pallas kernels for 0%

profile of v1, /device:TPU:0, one launch (start us, length us, event | category | flops | bytes accessed | tf_op | source)
XLA Modules:
  0.0 1201.9 jit_solution(3492719368294546650)
XLA Ops:
  9.7 34.3 %gather_fusion = s32[6144]{0:T(1024)S(1)} fusion(s32[2048]{0:T(1024)S(1)} %bitcast.160, s32[6144]{0:T(1024)S(1)} %broadcast_clamp_fusion.1), kind=kCustom, calls=%fused_computation.clone | custom fusion | bytes 73728 | tf_op jit(solution)/shard_map/jit(_take)/gather | solution.py:108
  44.6 23.0 %scatter_custom_fusion = s32[6144]{0:T(1024)S(1)} fusion(s32[6144]{0:T(1024)S(1)} %reshape.282, s32[6144]{0:T(1024)S(1)} %reshape.284, s32[]{:T(128)} %constant.20.clone.1), kind=kCustom, calls=%fused_computation.120 | custom fusion | bytes 24580
  67.9 34.3 %gather_fusion.1 = s32[6144]{0:T(1024)S(1)} fusion(s32[2048]{0:T(1024)S(1)} %convert_reduce_fusion.4, s32[6144]{0:T(1024)S(1)} %broadcast_clamp_fusion), kind=kCustom, calls=%fused_computation.2.clone | custom fusion | bytes 73728 | tf_op jit(solution)/shard_map/jit(_take)/gather | solution.py:112
  102.4 12.1 %all_gather.34 = bf16[192,768]{0,1:T(8,128)(2,1)} all-gather(bf16[192,96]{0,1:T(8,128)(2,1)S(1)} %copy.132), channel_id=1, replica_groups=mesh['dp'=8,'tensor'=4] {'dp'}, dimensions={1}, use_global_device_ids=true | all-gather | bytes 331776 | tf_op jit(solution)/shard_map/all_gather | solution.py:101
  114.5 10.5 all_gather.31
  124.9 9.6 all_gather.32
  134.6 9.7 all_gather.33
  144.3 3.1 fusion.8
  148.3 32.3 %gather_fusion.4 = bf16[6144,64]{1,0:T(8,128)(2,1)S(1)} fusion(bf16[3,2048,64]{2,1,0:T(8,128)(2,1)S(1)} %bitcast.163, s32[6144]{0:T(1024)S(1)} %reshape.300), kind=kCustom, calls=%fused_computation.4.clone | custom fusion | bytes 1622016 | tf_op jit(solution)/shard_map/jit(take_along_axis)/gather | solution.py:50
  182.0 3.1 convolution_convert_fusion.4
  186.0 32.3 %gather_fusion.3 = bf16[6144,64]{1,0:T(8,128)(2,1)S(1)} fusion(bf16[3,2048,64]{2,1,0:T(8,128)(2,1)S(1)} %bitcast.164, s32[6144]{0:T(1024)S(1)} %reshape.300), kind=kCustom, calls=%fused_computation.3.clone | custom fusion | bytes 1622016 | tf_op jit(solution)/shard_map/jit(take_along_axis)/gather | solution.py:50
  219.7 3.1 fusion.7
  223.7 32.3 %gather_fusion.2 = bf16[6144,64]{1,0:T(8,128)(2,1)S(1)} fusion(bf16[3,2048,64]{2,1,0:T(8,128)(2,1)S(1)} %bitcast.165, s32[6144]{0:T(1024)S(1)} %reshape.300), kind=kCustom, calls=%fused_computation.1.clone | custom fusion | bytes 1622016 | tf_op jit(solution)/shard_map/jit(take_along_axis)/gather | solution.py:50
  256.7 1.6 select_bitcast_fusion.3
  258.3 3.2 fusion.46
  264.6 32.3 %gather_fusion.5 = bf16[6144,64]{1,0:T(8,128)(2,1)S(1)} fusion(bf16[3,2048,64]{2,1,0:T(8,128)(2,1)S(1)} %bitcast.166, s32[6144]{0:T(1024)S(1)} %reshape.312), kind=kCustom, calls=%fused_computation.5.clone | custom fusion | bytes 1622016 | tf_op jit(solution)/shard_map/jit(take_along_axis)/gather | solution.py:57
  298.6 2.7 convolution_convert_fusion.2
  302.2 59.9 %reduce-scatter.19.cloned.1.call-done = bf16[512,768]{1,0:T(8,128)(2,1)} async-done(((bf16[2048,768]{1,0:T(8,128)(2,1)}), bf16[512,768]{1,0:T(8,128)(2,1)}) %reduce-scatter.19.cloned.1.call-update) | async-done | bytes 786448 | tf_op jit(solution)/shard_map/reduce_scatter | solution.py:130
  362.1 1.5 fusion.15
  363.6 1.6 multiply_reduce_fusion.4
  367.3 62.8 %all-gather.9.cloned.1.call-done = bf16[2048,768]{1,0:T(8,128)(2,1)} async-done(((bf16[512,768]{1,0:T(8,128)(2,1)}), bf16[2048,768]{1,0:T(8,128)(2,1)}) %all-gather.9.cloned.1.call-update) | async-done | bytes 3145744 | tf_op jit(solution)/shard_map/all_gather | solution.py:136
  430.1 9.7 multiply_convert_fusion
  439.8 14.6 %all-gather.13.cloned.1.call-done = bf16[768,768]{0,1:T(8,128)(2,1)} async-done(((bf16[768,96]{0,1:T(8,128)(2,1)}), bf16[768,768]{0,1:T(8,128)(2,1)}) %all-gather.13.cloned.1.call-update) | async-done | bytes 1179664 | tf_op jit(solution)/shard_map/all_gather | solution.py:103
  454.4 6.5 convolution_convert_fusion.1
  461.0 60.3 %reduce-scatter.21.cloned.1.call-done = bf16[512,768]{1,0:T(8,128)(2,1)} async-done(((bf16[2048,768]{1,0:T(8,128)(2,1)}), bf16[512,768]{1,0:T(8,128)(2,1)}) %reduce-scatter.21.cloned.1.call-update) | async-done | bytes 786448 | tf_op jit(solution)/shard_map/reduce_scatter | solution.py:139
  521.3 1.9 fusion.45
  524.3 2.7 fusion.44
  528.3 63.3 %all-gather.15.cloned.1.call-done = bf16[2048,768]{1,0:T(8,128)(2,1)} async-done(((bf16[512,768]{1,0:T(8,128)(2,1)}), bf16[2048,768]{1,0:T(8,128)(2,1)}) %all-gather.15.cloned.1.call-update) | async-done | bytes 3145744 | tf_op jit(solution)/shard_map/all_gather | solution.py:148
  591.6 8.8 convert_reduce_fusion
  600.4 1.6 copy-done.52
  602.1 4.0 convolution_convert_fusion
  606.2 59.0 %reduce-scatter.23.cloned.1.call-done = bf16[512,768]{1,0:T(8,128)(2,1)} async-done(((bf16[2048,768]{1,0:T(8,128)(2,1)}), bf16[512,768]{1,0:T(8,128)(2,1)}) %reduce-scatter.23.cloned.1.call-update) | async-done | bytes 786448 | tf_op jit(solution)/shard_map/reduce_scatter | solution.py:152
  665.2 2.2 multiply_reduce_fusion.1
  671.2 63.1 %all-gather.17.cloned.1.call-done = bf16[2048,768]{1,0:T(8,128)(2,1)} async-done(((bf16[512,768]{1,0:T(8,128)(2,1)}), bf16[2048,768]{1,0:T(8,128)(2,1)}) %all-gather.17.cloned.1.call-update) | async-done | bytes 3145744 | tf_op jit(solution)/shard_map/all_gather | solution.py:164
  734.3 3.1 convolution_convert_fusion.3
  738.2 60.6 %gather_fusion.6 = bf16[6144,64]{1,0:T(8,128)(2,1)} fusion(bf16[3,2048,64]{2,1,0:T(8,128)(2,1)S(1)} %bitcast.161, s32[6144]{0:T(1024)S(1)} %reshape.300), kind=kCustom, calls=%fused_computation.6.clone | custom fusion | bytes 1622016 | tf_op jit(solution)/shard_map/jit(take_along_axis)/gather | solution.py:50
  798.8 2.6 copy.134
  801.4 4.3 convolution_convert_fusion.6
  807.9 2.1 multiply_convert_fusion.2
  811.4 2.2 convolution_bitcast_fusion
  814.8 32.3 %gather_fusion.9 = bf16[6144,64]{1,0:T(8,128)(2,1)S(1)} fusion(bf16[3,2048,64]{2,1,0:T(8,128)(2,1)S(1)} %bitcast.167, s32[6144]{0:T(1024)S(1)} %reshape.312), kind=kCustom, calls=%fused_computation.9.clone | custom fusion | bytes 1622016 | tf_op jit(solution)/shard_map/jit(take_along_axis)/gather | solution.py:57
  848.5 1.8 copy.160
  850.3 32.3 %gather_fusion.7 = bf16[6144,64]{1,0:T(8,128)(2,1)S(1)} fusion(bf16[3,2048,64]{2,1,0:T(8,128)(2,1)S(1)} %bitcast.168, s32[6144]{0:T(1024)S(1)} %reshape.312), kind=kCustom, calls=%fused_computation.7.clone | custom fusion | bytes 1622016 | tf_op jit(solution)/shard_map/jit(take_along_axis)/gather | solution.py:57
  884.0 1.8 copy.161
  885.8 32.3 %gather_fusion.8 = bf16[6144,64]{1,0:T(8,128)(2,1)S(1)} fusion(bf16[3,2048,64]{2,1,0:T(8,128)(2,1)S(1)} %bitcast.162, s32[6144]{0:T(1024)S(1)} %reshape.312), kind=kCustom, calls=%fused_computation.8.clone | custom fusion | bytes 1622016 | tf_op jit(solution)/shard_map/jit(take_along_axis)/gather | solution.py:57
  922.7 2.8 add_convert_fusion
  925.5 1.8 copy-done.46
  927.3 6.0 fusion.49
  933.7 7.1 fusion.50
  940.8 2.8 convolution_bitcast_fusion.1
  943.6 2.2 copy.167
  945.9 2.8 convolution_bitcast_fusion.3
  948.7 2.2 copy.163
  951.0 2.8 convolution_bitcast_fusion.2
  953.7 2.3 copy.165
  957.0 19.2 %all-reduce.1 = (f32[768]{0:T(1024)S(1)}, f32[768]{0:T(1024)S(1)}, f32[768]{0:T(1024)S(1)}, f32[768]{0:T(1024)S(1)}, f32[768]{0:T(1024)S(1)}, /*index=5*/f32[307...) all-reduce(f32[768]{0:T(1024)S(1)} %dynamic_update_slice.9, ...), channel_id=1, replica_groups=mesh['dp'=8,'tensor'=4] {'tensor'}, use_global_device_ids=true, to_apply=%region_20.23 | all-reduce | flops 9216 | bytes 73728 | tf_op jit(solution)/shard_map/psum | solution.py:13
  976.2 23.7 %all-reduce = (f32[768]{0:T(1024)S(1)}, f32[768]{0:T(1024)S(1)}, f32[768]{0:T(1024)}, f32[768]{0:T(1024)}, f32[768]{0:T(1024)}, /*index=5*/f32[3072]{0:T(1024)S(1)}, f32[768]{0:T(1024)}, f32[768]{0:T(1024)}, f32[768]{0:T(1024)}) all-reduce(f32[768]{0:T(1024)S(1)} %get-tuple-element.103, ...), channel_id=1, replica_groups=mesh['dp'=8,'tensor'=4] {'dp'}, use_global_device_ids=true, to_apply=%region_21.24 | all-reduce | flops 9216 | bytes 73728 | tf_op jit(solution)/shard_map/psum | solution.py:13
  1001.8 1.6 copy.170
  1003.5 2.5 convert_add_fusion
  1006.0 26.1 %reduce-scatter.27.cloned.1.call-done = f32[96,768]{1,0:T(8,128)} async-done(((f32[768,768]{1,0:T(8,128)}), f32[96,768]{1,0:T(8,128)}) %reduce-scatter.27.cloned.1.call-update) | async-done | bytes 294928 | tf_op jit(solution)/shard_map/reduce_scatter | solution.py:255
  1032.1 46.5 %reduce-scatter.29.cloned.1.call-done = f32[768,96]{0,1:T(8,128)} async-done(((f32[768,768]{0,1:T(8,128)}), f32[768,96]{0,1:T(8,128)}) %reduce-scatter.29.cloned.1.call-update) | async-done | bytes 294928 | tf_op jit(solution)/shard_map/reduce_scatter | solution.py:256
  1078.6 38.7 %reduce-scatter.35.cloned.1.call-done = f32[96,192]{1,0:T(8,128)} async-done(((f32[768,192]{1,0:T(8,128)}), f32[96,192]{1,0:T(8,128)}) %reduce-scatter.35.cloned.1.call-update) | async-done | bytes 73744
  1117.3 38.6 %reduce-scatter.31.cloned.1.call-done = f32[96,192]{1,0:T(8,128)} async-done(((f32[768,192]{1,0:T(8,128)}), f32[96,192]{1,0:T(8,128)}) %reduce-scatter.31.cloned.1.call-update) | async-done | bytes 73744
  1155.9 38.7 %reduce-scatter.33.cloned.1.call-done = f32[96,192]{1,0:T(8,128)} async-done(((f32[768,192]{1,0:T(8,128)}), f32[96,192]{1,0:T(8,128)}) %reduce-scatter.33.cloned.1.call-update) | async-done | bytes 73744
  (217 shorter events, 38.7 us)
Async XLA Ops:
  8.0 1.6 copy-start
  8.0 136.3 %all-gather.7.cloned.1.call-start = ((), (), s32[]{:S(2)}) async-start(), calls=%async_computation.10 | async-start | bytes 3932160 | tf_op jit(solution)/shard_map/all_gather | solution.py:115
  8.8 353.3 %reduce-scatter.19.cloned.1.call-start = ((), (), s32[]{:S(2)}) async-start(), calls=%async_computation.11 | async-start | bytes 3932160 | tf_op jit(solution)/shard_map/reduce_scatter | solution.py:130
  9.6 34.4 %copy-start.34 = (s32[1,3,2048]{2,0,1:T(1,128)S(1)}, s32[1,3,2048]{2,0,1:T(1,128)}, u32[]{:S(2)}) copy-start(s32[1,3,2048]{2,0,1:T(1,128)} %param.28) | copy-start | bytes 73732
  9.6 34.5 %copy-start.44 = (s32[2]{0:T(128)S(1)}, s32[2]{0:T(128)}, u32[]{:S(2)}) copy-start(s32[2]{0:T(128)} %constant.77) | copy-start | bytes 28
  9.7 34.5 %copy-start.45 = (s32[2]{0:T(128)S(1)}, s32[2]{0:T(128)}, u32[]{:S(2)}) copy-start(s32[2]{0:T(128)} %constant.80) | copy-start | bytes 28
  9.7 34.7 %copy-start.51 = (s32[1,3]{1,0:T(1,128)S(1)}, s32[1,3]{1,0:T(1,128)}, u32[]{:S(2)}) copy-start(s32[1,3]{1,0:T(1,128)} %param.26) | copy-start | bytes 40
  67.9 34.4 %copy-start.39 = (bf16[192,96]{1,0:T(8,128)(2,1)S(1)}, bf16[192,96]{1,0:T(8,128)(2,1)}, u32[]{:S(2)}) copy-start(bf16[192,96]{1,0:T(8,128)(2,1)} %param.34) | copy-start | bytes 110596
  67.9 46.6 %copy-start.36 = (bf16[96,192]{1,0:T(8,128)(2,1)S(1)}, bf16[96,192]{1,0:T(8,128)(2,1)}, u32[]{:S(2)}) copy-start(bf16[96,192]{1,0:T(8,128)(2,1)} %param.29) | copy-start | bytes 110596
  67.9 57.0 %copy-start.37 = (bf16[96,192]{1,0:T(8,128)(2,1)S(1)}, bf16[96,192]{1,0:T(8,128)(2,1)}, u32[]{:S(2)}) copy-start(bf16[96,192]{1,0:T(8,128)(2,1)} %param.31) | copy-start | bytes 110596
  67.9 66.7 %copy-start.38 = (bf16[96,192]{1,0:T(8,128)(2,1)S(1)}, bf16[96,192]{1,0:T(8,128)(2,1)}, u32[]{:S(2)}) copy-start(bf16[96,192]{1,0:T(8,128)(2,1)} %param.32) | copy-start | bytes 110596
  67.9 76.4 %copy-start.49 = (f32[192]{0:T(256)S(1)}, f32[192]{0:T(256)}, u32[]{:S(2)}) copy-start(f32[192]{0:T(256)} %param.33) | copy-start | bytes 2308
  144.2 3.2 copy-start.31
  186.0 33.7 %copy-start.50 = (f32[192]{0:T(256)S(1)}, f32[192]{0:T(256)}, u32[]{:S(2)}) copy-start(f32[192]{0:T(256)} %param.30) | copy-start | bytes 2308
  258.3 3.9 copy-start.19
  258.3 3.9 copy-start.21
  258.3 3.9 copy-start.12
  261.5 1.7 copy-start.2
  296.9 1.7 copy-start.16
  298.6 63.5 %copy-start.5 = (bf16[512,768]{1,0:T(8,128)(2,1)S(1)}, bf16[512,768]{1,0:T(8,128)(2,1)}, u32[]{:S(2)}) copy-start(bf16[512,768]{1,0:T(8,128)(2,1)} %param.24) | copy-start | bytes 2359300
  298.6 63.5 %copy-start.33 = (f32[768]{0:T(1024)S(1)}, f32[768]{0:T(1024)}, u32[]{:S(2)}) copy-start(f32[768]{0:T(1024)} %param.35) | copy-start | bytes 9220
  301.3 63.9 %copy-start.35 = (f32[768]{0:T(1024)S(1)}, f32[768]{0:T(1024)}, u32[]{:S(2)}) copy-start(f32[768]{0:T(1024)} %param.36) | copy-start | bytes 9220
  301.3 63.9 %copy-start.41 = (f32[768]{0:T(1024)S(1)}, f32[768]{0:T(1024)}, u32[]{:S(2)}) copy-start(f32[768]{0:T(1024)} %param.37) | copy-start | bytes 9220
  301.4 65.9 %all-gather.11.cloned.1.call-start = ((), (), s32[]{:S(2)}) async-start(), calls=%async_computation.13 | async-start | bytes 1327104 | tf_op jit(solution)/shard_map/all_gather | solution.py:102
  301.9 128.1 %copy-start.48 = (f32[768]{0:T(1024)S(1)}, f32[768]{0:T(1024)}, u32[]{:S(2)}) copy-start(f32[768]{0:T(1024)} %param.39) | copy-start | bytes 9220
  301.9 128.1 %all-gather.9.cloned.1.call-start = ((), (), s32[]{:S(2)}) async-start(), calls=%async_computation.12 | async-start | bytes 3932160 | tf_op jit(solution)/shard_map/all_gather | solution.py:136
  362.1 3.2 copy-start.6
  366.6 87.8 %all-gather.13.cloned.1.call-start = ((), (), s32[]{:S(2)}) async-start(), calls=%async_computation.14 | async-start | bytes 1327104 | tf_op jit(solution)/shard_map/all_gather | solution.py:103
  367.2 154.1 %reduce-scatter.21.cloned.1.call-start = ((), (), s32[]{:S(2)}) async-start(), calls=%async_computation.15 | async-start | bytes 3932160 | tf_op jit(solution)/shard_map/reduce_scatter | solution.py:139
  460.9 60.4 %copy-start.43 = (f32[768]{0:T(1024)S(1)}, f32[768]{0:T(1024)}, u32[]{:S(2)}) copy-start(f32[768]{0:T(1024)} %param.41) | copy-start | bytes 9220
  461.0 62.6 %copy-start.18 = (bf16[512,768]{1,0:T(8,128)(2,1)S(1)}, bf16[512,768]{1,0:T(8,128)(2,1)}, u32[]{:S(2)}) copy-start(bf16[512,768]{1,0:T(8,128)(2,1)} %param.25) | copy-start | bytes 2359300
  461.0 62.6 %copy-start.40 = (f32[768]{0:T(1024)S(1)}, f32[768]{0:T(1024)}, u32[]{:S(2)}) copy-start(f32[768]{0:T(1024)} %param.42) | copy-start | bytes 9220
  461.0 63.3 %copy-start.42 = (f32[768]{0:T(1024)S(1)}, f32[768]{0:T(1024)}, u32[]{:S(2)}) copy-start(f32[768]{0:T(1024)} %param.43) | copy-start | bytes 9220
  461.0 130.6 %all-gather.15.cloned.1.call-start = ((), (), s32[]{:S(2)}) async-start(), calls=%async_computation.16 | async-start | bytes 3932160 | tf_op jit(solution)/shard_map/all_gather | solution.py:148
  528.0 137.1 %reduce-scatter.23.cloned.1.call-start = ((), (), s32[]{:S(2)}) async-start(), calls=%async_computation.17 | async-start | bytes 3932160 | tf_op jit(solution)/shard_map/reduce_scatter | solution.py:152
  591.6 10.5 copy-start.47
  600.4 1.7 copy-start.52
  606.1 128.2 %all-gather.17.cloned.1.call-start = ((), (), s32[]{:S(2)}) async-start(), calls=%async_computation.18 | async-start | bytes 3932160 | tf_op jit(solution)/shard_map/all_gather | solution.py:164
  665.2 2.3 copy-start.24
  668.4 1.2 copy-start.7
  668.4 65.9 %copy-start.17 = (bf16[192,768]{0,1:T(8,128)(2,1)S(1)}, bf16[192,768]{0,1:T(8,128)(2,1)}, u32[]{:S(2)}) copy-start(bf16[192,768]{0,1:T(8,128)(2,1)} %all_gather.34) | copy-start | bytes 884740
  670.7 331.1 %reduce-scatter.37.cloned.1.call-start = ((), (), s32[]{:S(2)}) async-start(), calls=%async_computation.25 | async-start | bytes 884736
  798.8 6.9 copy-start.3
  801.4 4.3 copy-start.13
  801.4 4.3 copy-start.14
  807.9 2.1 copy-start.20
  807.9 3.6 copy-start.25
  807.9 3.6 copy-start.29
  811.4 2.5 copy-start.23
  813.7 189.8 %reduce-scatter.25.cloned.1.call-start = ((), (), s32[]{:S(2)}) async-start(), calls=%async_computation.19 | async-start | bytes 3932160 | tf_op jit(solution)/shard_map/reduce_scatter | solution.py:194
  918.9 1.3 copy-start.9
  919.1 1.2 copy-start.26
  919.1 1.4 copy-start.27
  921.1 1.5 copy-start.10
  921.1 1.5 copy-start.11
  925.4 1.9 copy-start.46
  925.5 106.7 %reduce-scatter.27.cloned.1.call-start = ((), (), s32[]{:S(2)}) async-start(), calls=%async_computation.20 | async-start | bytes 2654208 | tf_op jit(solution)/shard_map/reduce_scatter | solution.py:255
  933.4 7.4 copy-start.4
  933.4 145.2 %reduce-scatter.29.cloned.1.call-start = ((), (), s32[]{:S(2)}) async-start(), calls=%async_computation.21 | async-start | bytes 2654208 | tf_op jit(solution)/shard_map/reduce_scatter | solution.py:256
  940.7 176.6 %reduce-scatter.35.cloned.1.call-start = ((), (), s32[]{:S(2)}) async-start(), calls=%async_computation.24 | async-start | bytes 884736
  945.8 210.1 %reduce-scatter.31.cloned.1.call-start = ((), (), s32[]{:S(2)}) async-start(), calls=%async_computation.22 | async-start | bytes 884736
  950.9 243.7 %reduce-scatter.33.cloned.1.call-start = ((), (), s32[]{:S(2)}) async-start(), calls=%async_computation.23 | async-start | bytes 884736
  951.0 243.6 %copy-start.1 = (s32[1,2048]{1,0:T(1,128)S(1)}, s32[1,2048]{1,0:T(1,128)}, u32[]{:S(2)}) copy-start(s32[1,2048]{1,0:T(1,128)} %param.27) | copy-start | bytes 24580
  953.7 49.7 %copy-start.8 = (f32[512,768]{1,0:T(8,128)S(1)}, f32[512,768]{1,0:T(8,128)}, u32[]{:S(2)}) copy-start(f32[512,768]{1,0:T(8,128)} %copy-done.7) | copy-start | bytes 4718596
  (5 other events, 5.2 us)
Sparse Core Ops, SparseCore 0:
  10.4 66.1 all-gather.6
  301.5 60.5 reduce-scatter.18
  528.2 63.4 all-gather.14
  670.9 63.4 all-gather.16
Sparse Core Ops, SparseCore 1:
  303.7 24.1 all-gather.10
  366.7 63.3 all-gather.8
  431.8 22.5 all-gather.12
  461.0 60.2 reduce-scatter.20
  606.2 58.9 reduce-scatter.22
  813.8 33.6 reduce-scatter.36
  925.5 60.4 reduce-scatter.24
  989.8 42.3 reduce-scatter.26
  1036.3 42.3 reduce-scatter.28
  1082.4 34.9 reduce-scatter.34
  1120.9 34.9 reduce-scatter.30
  1159.6 34.9 reduce-scatter.32
